TPU v7x, 256 devices: a whole 4x4x8 slice. The times are simulated.
256 devices in a mesh: seq: 32 (over x, y, core), dp: 8 (over z).
Axes of the slice: x: 4, y: 4, z: 8, core: 2. Of those that a mesh axis runs over, the one named last changes fastest.
Arguments:
- queries: bfloat16 [8, 16384, 2048], P('dp', 'seq'), may hold values from -5 to 5
- keys: bfloat16 [8, 16384, 2048], P('dp', 'seq'), may hold values from -5 to 5
- values: bfloat16 [8, 16384, 2048], P('dp', 'seq'), may hold values from -8 to 8
- out_weight: bfloat16 [2048, 4096], P(None, 'dp'), may hold values from -0.125 to 0.125
Outputs:
- projected: bfloat16 [8, 16384, 4096], P('dp', 'seq')
All inputs are finite; a program needn't handle non-finite values.
Results may differ from a plain program's by a relative error of at most 0.0061.
Values may be sent and summed in bfloat16 or wider, within the bound.
No kernel may reach another device: no remote copies, remote signals or barrier semaphores. Data moves between devices by JAX's collectives and lax.ppermute only.
A program may use at most 192 MiB of HBM per device.

v0:
```python
import math
import jax
import jax.numpy as jnp
from jax import lax
from jax.sharding import PartitionSpec as P

CHANNEL_WIDTH = 128
SEGMENT_LENGTH = 256


def prefix(value, axis, join, neutral):
    count, mine = (lax.axis_size(axis), lax.axis_index(axis))
    pieces = jax.tree.map(lambda part: lax.all_gather(part, axis), value)
    subtotal = jax.tree.map(
        lambda part, zero: jnp.full_like(part, 0) + jnp.asarray(zero, part.dtype), value, neutral
    )

    def turn(position, subtotal):
        longer = join(subtotal, jax.tree.map(lambda part: part[position], pieces))
        return jax.tree.map(lambda new, old: jnp.where(position < mine, new, old), longer, subtotal)

    return lax.fori_loop(0, count - 1, turn, subtotal)


def shifted(block, axis, distance):
    devices = range(lax.axis_size(axis))
    route = [(i - distance, i) for i in devices if i - distance in devices]
    return lax.ppermute(block, axis, route)


def add_pair(earlier_pair, later_pair):
    return (earlier_pair[0] + later_pair[0], earlier_pair[1] + later_pair[1])


def per_device(queries, keys, values, out_weight):
    local_rows = queries.shape[1]
    feature_width = queries.shape[2]
    head_count = feature_width // CHANNEL_WIDTH
    local_blocks = local_rows // SEGMENT_LENGTH
    shard_count = lax.axis_size("seq")
    shard_index = lax.axis_index("seq")
    total_blocks = local_blocks * shard_count
    first_block = shard_index * local_blocks
    softmax_multiplier = 1.0 / math.sqrt(CHANNEL_WIDTH)
    faraway_offset_bias = math.log(SEGMENT_LENGTH)
    own_queries = queries[0]
    own_keys = keys[0]
    own_values = values[0]
    span_address_means = jnp.mean(
        own_keys.reshape(local_blocks, SEGMENT_LENGTH, feature_width), axis=1, dtype=jnp.float32
    ).astype(jnp.bfloat16)
    value_means = jnp.mean(
        own_values.reshape(local_blocks, SEGMENT_LENGTH, feature_width), axis=1, dtype=jnp.float32
    ).astype(jnp.bfloat16)
    empty_buffer = jnp.zeros((total_blocks, feature_width), jnp.bfloat16)
    slot_keys = lax.dynamic_update_slice_in_dim(empty_buffer, span_address_means, first_block, 0)
    slot_values = lax.dynamic_update_slice_in_dim(empty_buffer, value_means, first_block, 0)
    far_keys, far_values = prefix(
        (slot_keys, slot_values), "seq", add_pair, (empty_buffer, empty_buffer)
    )
    prev_keys, prev_values = shifted(
        (own_keys[local_rows - SEGMENT_LENGTH :], own_values[local_rows - SEGMENT_LENGTH :]),
        "seq",
        1,
    )
    near_keys = jnp.concatenate([prev_keys, own_keys], axis=0)
    near_values = jnp.concatenate([prev_values, own_values], axis=0)
    far_k = far_keys.reshape(total_blocks, head_count, CHANNEL_WIDTH)
    far_v = far_values.reshape(total_blocks, head_count, CHANNEL_WIDTH)
    far_index = jnp.arange(total_blocks, dtype=jnp.int32)
    group_rows = SEGMENT_LENGTH * math.gcd(local_blocks, max(1, 512 // SEGMENT_LENGTH))
    request_vectors = own_queries.reshape(group_rows, head_count, CHANNEL_WIDTH)
    address_vectors = near_keys.reshape(group_rows + SEGMENT_LENGTH, head_count, CHANNEL_WIDTH)
    value_rows = near_values.reshape(group_rows + SEGMENT_LENGTH, head_count, CHANNEL_WIDTH)
    query_local = 0 + jnp.arange(group_rows, dtype=jnp.int32)
    key_local = 0 - SEGMENT_LENGTH + jnp.arange(group_rows + SEGMENT_LENGTH, dtype=jnp.int32)
    query_blk = query_local // SEGMENT_LENGTH
    key_blk = key_local // SEGMENT_LENGTH
    within_block = (key_blk[None, :] == query_blk[:, None]) & (
        key_local[None, :] <= query_local[:, None]
    )
    preceding_segment = (key_blk[None, :] == query_blk[:, None] - 1) & (
        (key_blk[None, :] >= 0) | (shard_index > 0)
    )
    adjacent_similarity = (
        jnp.einsum(
            "qhd,khd->hqk", request_vectors, address_vectors, preferred_element_type=jnp.float32
        )
        * softmax_multiplier
    )
    adjacent_similarity = jnp.where(
        (within_block | preceding_segment)[None], adjacent_similarity, -jnp.inf
    )
    query_global = first_block + query_blk
    faraway_similarity = (
        jnp.einsum("qhd,jhd->hqj", request_vectors, far_k, preferred_element_type=jnp.float32)
        * softmax_multiplier
        + faraway_offset_bias
    )
    faraway_similarity = jnp.where(
        (far_index[None, :] < query_global[:, None] - 1)[None], faraway_similarity, -jnp.inf
    )
    row_max = jnp.maximum(
        jnp.max(adjacent_similarity, axis=-1), jnp.max(faraway_similarity, axis=-1)
    )[..., None]
    near_w = jnp.exp(adjacent_similarity - row_max)
    far_w = jnp.exp(faraway_similarity - row_max)
    row_total = jnp.sum(near_w, axis=-1, keepdims=True) + jnp.sum(far_w, axis=-1, keepdims=True)
    near_p = (near_w / row_total).astype(jnp.bfloat16)
    far_p = (far_w / row_total).astype(jnp.bfloat16)
    attended = jnp.einsum("hqk,khd->qhd", near_p, value_rows, preferred_element_type=jnp.float32)
    attended = attended + jnp.einsum(
        "hqj,jhd->qhd", far_p, far_v, preferred_element_type=jnp.float32
    )
    pieces = attended.astype(jnp.bfloat16).reshape(group_rows, feature_width)
    projected = jnp.dot(
        pieces,
        lax.all_gather(out_weight, "dp", axis=1, tiled=True),
        preferred_element_type=jnp.float32,
    ).astype(jnp.bfloat16)
    return projected[None]


def solution(mesh):
    return jax.shard_map(
        per_device,
        mesh=mesh,
        in_specs=(P("dp", "seq", None), P("dp", "seq", None), P("dp", "seq", None), P(None, "dp")),
        out_specs=P("dp", "seq", None),
        check_vma=False,
    )
```

profile of v0, /device:TPU:1, one launch (start us, length us, event | category | flops | bytes accessed | tf_op | source)
XLA Modules:
  0.0 340.8 jit_solution(379502660158891560)
XLA Ops:
  6.5 2.1 convert_reduce_fusion.1
  11.4 3.9 %copy.25 = bf16[1,512,2048]{1,2,0:T(8,128)(2,1)} copy(bf16[1,512,2048]{2,1,0:T(8,128)(2,1)} %param.7) | data formatting | bytes 4194304 | tf_op args[1]
  15.4 2.3 slice_bitcast_fusion
  17.7 4.6 %collective-permute-start.1 = (bf16[256,2048]{0,1:T(8,128)(2,1)}, bf16[256,2048]{0,1:T(8,128)(2,1)}, u32[]{:S(2)}, u32[]{:S(2)}) collective-permute-start(bf16[256,2048]{0,1:T(8,128)(2,1)} %slice_bitcast_fusion), channel_id=1, source_target_pairs={{0,8},{8,16},{16,24},{24,32},{32,40},{40,48},{48,56},{56,64},{64,7... | collective-permute-start | bytes 3145736 | tf_op jit(solution)/shard_map/ppermute | solution.py:28
  23.3 1.9 collective-permute-start
  25.2 2.5 copy.24
  27.7 3.7 %copy.37 = bf16[64,8,16,128]{3,2,1,0:T(8,128)(2,1)} copy(bf16[64,8,16,128]{3,1,2,0:T(8,128)(2,1)} %bitcast.68) | data formatting | bytes 4194304
  31.4 2.4 copy.28
  34.7 3.3 collective-permute-done.1
  38.1 2.3 copy.27
  40.3 9.4 %collective-permute-done = bf16[256,2048]{1,0:T(8,128)(2,1)} collective-permute-done((bf16[256,2048]{1,0:T(8,128)(2,1)}, bf16[256,2048]{1,0:T(8,128)(2,1)}, u32[]{:S(2)}, u32[]{:S(2)}) %collective-permute-start) | collective-permute-done | bytes 1048608 | tf_op jit(solution)/shard_map/ppermute | solution.py:28
  49.7 2.3 copy.23
  52.0 12.3 %fusion.1 = (f32[16,512]{1,0:T(8,128)S(1)}, f32[16,768,512]{2,1,0:T(8,128)}) fusion(pred[512,768]{0,1:T(8,128)(4,1)S(1)} %fusion.20, bf16[512,16,128]{2,1,0:T(8,128)(2,1)S(1)} %bitcast.70, bf16[512,16,128]{2,0,1:T(8,128)(2,1)} %copy.28, bf16[256,16,128]{2,0,1:T(8,128)(2,1)} %copy.27), kind=kOutput, calls=%fused_computation.6 | convolution fusion | flops 1635770368 | bytes 30834688 | tf_op jit(solution)/shard_map/qhd,khd->hqk/dot_general | solution.py:86
  64.3 21.8 %all-gather.4.cloned.1.call-done = bf16[32,64,2048]{2,1,0:T(8,128)(2,1)} async-done(((bf16[1,64,2048]{2,1,0:T(8,128)(2,1)}), bf16[32,64,2048]{2,1,0:T(8,128)(2,1)}) %all-gather.4.cloned.1.call-update) | async-done | bytes 8388624 | tf_op jit(solution)/shard_map/all_gather | solution.py:13
  86.1 60.0 %all-gather.6.cloned.1.call-done = bf16[32,64,2048]{2,1,0:T(8,128)(2,1)} async-done(((bf16[1,64,2048]{2,1,0:T(8,128)(2,1)}), bf16[32,64,2048]{2,1,0:T(8,128)(2,1)}) %all-gather.6.cloned.1.call-update) | async-done | bytes 8388624 | tf_op jit(solution)/shard_map/all_gather | solution.py:13
  146.2 39.2 %while.16 = (s32[]{:T(128)}, bf16[64,2048]{1,0:T(8,128)(2,1)S(1)}, bf16[64,2048]{1,0:T(8,128)(2,1)S(1)}, s32[]{:T(128)}, bf16[32,64,2048]{2,1,0:T(8,128)(2,1)}, ...) while((s32[]{:T(128)}, bf16[64,2048]{1,0:T(8,128)(2,1)S(1)}, ...), condition=%wide.region_4.5_spmd.clone, body=%wide.region_3.4_spmd.clone.sunk | while | flops 786436 | bytes 1572973 | solution.py:22
  147.4 1.2 add_select_fusion.5
  148.7 1.2 add_select_fusion.5
  149.9 1.2 add_select_fusion.5
  151.2 1.2 add_select_fusion.5
  152.5 1.2 add_select_fusion.5
  155.0 1.2 add_select_fusion.5
  156.2 1.2 add_select_fusion.5
  158.8 1.3 add_select_fusion.5
  160.1 1.3 add_select_fusion.5
  161.4 1.2 add_select_fusion.5
  163.9 1.2 add_select_fusion.5
  165.2 1.2 add_select_fusion.5
  166.4 1.2 add_select_fusion.5
  167.7 1.2 add_select_fusion.5
  168.9 1.2 add_select_fusion.5
  170.2 1.2 add_select_fusion.5
  171.5 1.2 add_select_fusion.5
  172.7 1.2 add_select_fusion.5
  174.0 1.2 add_select_fusion.5
  175.3 1.2 add_select_fusion.5
  176.5 1.2 add_select_fusion.5
  177.8 1.2 add_select_fusion.5
  179.1 1.2 add_select_fusion.5
  180.3 1.2 add_select_fusion.5
  181.6 1.2 add_select_fusion.5
  182.9 1.2 add_select_fusion.5
  185.4 1.5 fusion.42
  187.3 11.3 %fusion = f32[16,512]{1,0:T(8,128)S(1)} fusion(f32[16,768,512]{2,1,0:T(8,128)} %get-tuple-element.153, f32[16,512]{1,0:T(8,128)S(1)} %max.7, pred[512,768]{0,1:T(8,128)(4,1)S(1)} %fusion.20), kind=kLoop, calls=%fused_computation.5 | loop fusion | flops 25157632 | bytes 25624576 | tf_op jit(solution)/shard_map/reduce_sum | solution.py:108
  198.5 2.8 fusion.21
  201.3 14.6 %add_convert_fusion = bf16[16,128,512]{2,1,0:T(8,128)(2,1)} fusion(f32[16,128,512]{2,1,0:T(8,128)} %fusion.21, f32[16,768,512]{2,1,0:T(8,128)} %get-tuple-element.153, f32[16,512]{1,0:T(8,128)S(1)} %add.130, f32[16,512]{1,0:T(8,128)S(1)} %max.7, pred[512,768]{0,1:T(8,128)(4,1)S(1)} %fusion.20, bf16[512,16,128]{0,2,1:T(8,128)(2,1)S(1)} %bitcast.69, ...), kind=kOutput, calls=%fused_computation.12 | convolution fusion | flops 1650458624 | bytes 35061760 | tf_op jit(solution)/shard_map/hqk,khd->qhd/dot_general | solution.py:111
  215.9 103.9 %all-gather.8.cloned.1.call-done = bf16[2048,4096]{1,0:T(8,128)(2,1)} async-done(((bf16[2048,512]{1,0:T(8,128)(2,1)}), bf16[2048,4096]{1,0:T(8,128)(2,1)}) %all-gather.8.cloned.1.call-update) | async-done | bytes 16777232 | tf_op jit(solution)/shard_map/all_gather | solution.py:118
  319.8 14.5 %fusion.3 = bf16[1,512,4096]{2,1,0:T(8,128)(2,1)} fusion(bf16[512,2048]{0,1:T(8,128)(2,1)} %bitcast.73, bf16[2048,4096]{1,0:T(8,128)(2,1)} %all-gather.8.cloned.1.call-done), kind=kOutput, calls=%fused_computation.9 | convolution fusion | flops 8592031744 | bytes 23068672 | tf_op jit(solution)/shard_map/dot_general | solution.py:116
  (40 shorter events, 11.2 us)
Async XLA Ops:
  6.5 3.0 copy-start
  6.5 79.6 %all-gather.4.cloned.1.call-start = ((), (), s32[]{:S(2)}) async-start(), calls=%async_computation | async-start | bytes 8650752 | tf_op jit(solution)/shard_map/all_gather | solution.py:13
  8.7 0.7 copy-start.5
  9.5 136.7 %all-gather.6.cloned.1.call-start = ((), (), s32[]{:S(2)}) async-start(), calls=%async_computation.1 | async-start | bytes 8650752 | tf_op jit(solution)/shard_map/all_gather | solution.py:13
  10.0 0.7 copy-start.4
  10.7 309.1 %all-gather.8.cloned.1.call-start = ((), (), s32[]{:S(2)}) async-start(), calls=%async_computation.2 | async-start | bytes 18874368 | tf_op jit(solution)/shard_map/all_gather | solution.py:118
  17.7 20.4 %collective-permute-start.1 = (bf16[256,2048]{0,1:T(8,128)(2,1)}, bf16[256,2048]{0,1:T(8,128)(2,1)}, u32[]{:S(2)}, u32[]{:S(2)}) collective-permute-start(bf16[256,2048]{0,1:T(8,128)(2,1)} %slice_bitcast_fusion), channel_id=1, source_target_pairs={{0,8},{8,16},{16,24},{24,32},{32,40},{40,48},{48,56},{56,64},{64,7... | collective-permute-start | bytes 3145736 | tf_op jit(solution)/shard_map/ppermute | solution.py:28
  23.3 26.4 %collective-permute-start = (bf16[256,2048]{1,0:T(8,128)(2,1)}, bf16[256,2048]{1,0:T(8,128)(2,1)}, u32[]{:S(2)}, u32[]{:S(2)}) collective-permute-start(bf16[256,2048]{1,0:T(8,128)(2,1)} %slice_bitcast_fusion.1), channel_id=1, source_target_pairs={{0,8},{8,16},{16,24},{24,32},{32,40},{40,48},{48,56},{56,64},{64,7... | collective-permute-start | bytes 3145736 | tf_op jit(solution)/shard_map/ppermute | solution.py:28
  27.7 3.7 %copy-start.1 = (bf16[1,512,2048]{1,2,0:T(8,128)(2,1)S(1)}, bf16[1,512,2048]{1,2,0:T(8,128)(2,1)}, u32[]{:S(2)}) copy-start(bf16[1,512,2048]{1,2,0:T(8,128)(2,1)} %copy.25) | copy-start | bytes 6291460
  33.8 18.2 %copy-start.3 = (bf16[64,8,16,128]{3,2,1,0:T(8,128)(2,1)S(1)}, bf16[64,8,16,128]{3,2,1,0:T(8,128)(2,1)}, u32[]{:S(2)}) copy-start(bf16[64,8,16,128]{3,2,1,0:T(8,128)(2,1)} %copy.37) | copy-start | bytes 6291460
  198.5 2.8 copy-start.2
Sparse Core Ops, SparseCore 0:
  9.9 76.2 all-gather.3
  88.7 57.4 all-gather.5
  148.0 171.7 all-gather.7
where the time goes:
time: 342 us; the launch traced here: 341 us
  waiting for transfers between devices  199 us (58%)
  other arithmetic  53.6 us (16%)
  matrix products  45.6 us (13%)
  local copies, waits for them, and re-layouts  21.8 us (6%)
  between operations  13.3 us (4%)
  starting transfers between devices  6.57 us (2%)
    all_gather x1, waiting for transfers between devices, per_device(): lax.all_gather(out_weight, 'dp', axis=1, tiled=True)  104 us
    all_gather x2, waiting for transfers between devices, prefix(): pieces = jax.tree.map(lambda part: lax.all_gather(part, axis), value)  81.8 us
    select_n x31, other arithmetic, turn(): jnp.where(position < mine, new, old)  38.5 us
    dot_general x1, matrix products, per_device(): jnp.einsum('hqk,khd->qhd', near_p, value_rows, preferred_element_type=jnp...  14.6 us
    dot_general x1, matrix products, per_device(): jnp.dot(pieces, lax.all_gather(out_weight, 'dp', axis=1, tiled=True), pre...  14.5 us
    ppermute x2, waiting for transfers between devices, shifted(): return lax.ppermute(block, axis, route)  12.7 us
    dot_general x1, matrix products, per_device(): jnp.einsum('qhd,khd->hqk', request_vectors, address_vectors, preferred_el...  12.3 us
    unnamed x15, local copies, waits for them, and re-layouts  11.5 us
  transfers between devices with their start and end apart: 5, of which 5 were waited for; matrix products, arithmetic and copies ran while one was open for 30% of the time, Pallas kernels for 0%

commit v1 on v0

--- a/solution.py
+++ b/solution.py
@@ -1,3 +1,4 @@
+import functools
 import math
 import jax
 import jax.numpy as jnp
@@ -6,6 +7,16 @@
 
 CHANNEL_WIDTH = 128
 SEGMENT_LENGTH = 256
+
+
+def find_the_point(vec, group_axis, in_dim):
+    oldest = jnp.concatenate(
+        lax.all_to_all(jnp.stack([vec] * lax.axis_size(group_axis)), group_axis, 0, 0), axis=in_dim
+    )
+    return oldest
+
+
+block_solve = functools.partial(find_the_point, group_axis="dp", in_dim=1)
 
 
 def prefix(value, axis, join, neutral):
@@ -113,11 +124,9 @@
         "hqj,jhd->qhd", far_p, far_v, preferred_element_type=jnp.float32
     )
     pieces = attended.astype(jnp.bfloat16).reshape(group_rows, feature_width)
-    projected = jnp.dot(
-        pieces,
-        lax.all_gather(out_weight, "dp", axis=1, tiled=True),
-        preferred_element_type=jnp.float32,
-    ).astype(jnp.bfloat16)
+    projected = jnp.dot(pieces, block_solve(out_weight), preferred_element_type=jnp.float32).astype(
+        jnp.bfloat16
+    )
     return projected[None]
 
 

time: 342 us -> 420 us (1.23)
  waiting for transfers between devices: 199 us -> 258 us
  local copies, waits for them, and re-layouts: 21.8 us -> 32.7 us
  starting transfers between devices: 6.57 us -> 15.2 us
    all_to_all x0 -> x1, waiting for transfers between devices: none -> 189 us  [find_the_point(): lax.all_to_all(jnp.stack([vec] * lax.axis_size(group_axis)), group_axis,...]
    all_gather x1 -> x0, waiting for transfers between devices: 104 us -> none  [per_device(): lax.all_gather(out_weight, 'dp', axis=1, tiled=True)]
    all_gather x2, waiting for transfers between devices: 81.8 us -> 44.3 us  [prefix(): pieces = jax.tree.map(lambda part: lax.all_gather(part, axis), value)]
    ppermute x2, waiting for transfers between devices: 12.7 us -> 25.1 us  [shifted(): return lax.ppermute(block, axis, route)]
    all_to_all x0 -> x1, starting transfers between devices: none -> 9 us  [find_the_point(): lax.all_to_all(jnp.stack([vec] * lax.axis_size(group_axis)), group_axis,...]
    another operation x0 -> x1, local copies, waits for them, and re-layouts: none -> 6.87 us  [find_the_point(): jnp.stack([vec] * lax.axis_size(group_axis))]
    unnamed x15 -> x16, local copies, waits for them, and re-layouts: 11.5 us -> 15.5 us
  transfers between devices with their start and end apart: 5 -> 5, of which waited for: 5 -> 4; matrix products, arithmetic and copies ran while one was open for 30% -> 27% of each run, Pallas kernels for 0% -> 0%
where the time goes in v1:
time: 420 us; the launch traced here: 419 us
  waiting for transfers between devices  258 us (61%)
  other arithmetic  53.3 us (13%)
  matrix products  45.3 us (11%)
  local copies, waits for them, and re-layouts  32.7 us (8%)
  starting transfers between devices  15.2 us (4%)
  between operations  13.6 us (3%)
    all_to_all x1, waiting for transfers between devices, find_the_point(): lax.all_to_all(jnp.stack([vec] * lax.axis_size(group_axis)), group_axis,...  189 us
    all_gather x2, waiting for transfers between devices, prefix(): pieces = jax.tree.map(lambda part: lax.all_gather(part, axis), value)  44.3 us
    select_n x31, other arithmetic, turn(): jnp.where(position < mine, new, old)  38.3 us
    ppermute x2, waiting for transfers between devices, shifted(): return lax.ppermute(block, axis, route)  25.1 us
    unnamed x16, local copies, waits for them, and re-layouts  15.5 us
    dot_general x1, matrix products, per_device(): jnp.dot(pieces, block_solve(out_weight), preferred_element_type=jnp.float32)  14.4 us
    dot_general x1, matrix products, per_device(): jnp.einsum('hqk,khd->qhd', near_p, value_rows, preferred_element_type=jnp...  14.3 us
    dot_general x1, matrix products, per_device(): jnp.einsum('qhd,khd->hqk', request_vectors, address_vectors, preferred_el...  12.4 us
  transfers between devices with their start and end apart: 5, of which 4 were waited for; matrix products, arithmetic and copies ran while one was open for 27% of the time, Pallas kernels for 0%

profile of v1, /device:TPU:1, one launch (start us, length us, event | category | flops | bytes accessed | tf_op | source)
XLA Modules:
  0.0 419.0 jit_solution(14634214453570480860)
XLA Ops:
  6.5 2.1 convert_reduce_fusion.1
  10.7 3.9 copy.35
  14.6 6.9 %stack.2 = bf16[8,2048,512]{1,2,0:T(8,128)(2,1)} broadcast(bf16[2048,512]{0,1:T(8,128)(2,1)} %copy.35), dimensions={1,2} | broadcast | bytes 18874368 | tf_op jit(solution)/shard_map/stack | solution.py:14
  21.5 9.0 %all-to-all-start = ((bf16[8,2048,512]{1,2,0:T(8,128)(2,1)}), bf16[8,2048,512]{1,2,0:T(8,128)(2,1)}, u32[]{:S(2)}, u32[]{:S(2)}) async-start(bf16[8,2048,512]{1,2,0:T(8,128)(2,1)} %stack.2), calls=%async_computation | async-start | bytes 33554432 | tf_op jit(solution)/shard_map/all_to_all | solution.py:14
  30.5 3.9 copy.26
  34.4 2.3 slice_bitcast_fusion
  36.7 4.0 collective-permute-start.1
  41.8 2.1 collective-permute-start
  43.9 2.5 copy.25
  46.5 3.7 copy.39
  50.2 2.4 copy.29
  53.5 4.9 %collective-permute-done.1 = bf16[256,2048]{0,1:T(8,128)(2,1)} collective-permute-done((bf16[256,2048]{0,1:T(8,128)(2,1)}, bf16[256,2048]{0,1:T(8,128)(2,1)}, u32[]{:S(2)}, u32[]{:S(2)}) %collective-permute-start.1) | collective-permute-done | bytes 1048608 | tf_op jit(solution)/shard_map/ppermute | solution.py:39
  58.4 2.2 copy.28
  60.6 20.3 %collective-permute-done = bf16[256,2048]{1,0:T(8,128)(2,1)} collective-permute-done((bf16[256,2048]{1,0:T(8,128)(2,1)}, bf16[256,2048]{1,0:T(8,128)(2,1)}, u32[]{:S(2)}, u32[]{:S(2)}) %collective-permute-start) | collective-permute-done | bytes 1048608 | tf_op jit(solution)/shard_map/ppermute | solution.py:39
  80.9 2.3 copy.24
  83.2 12.4 %fusion.1 = (f32[16,512]{1,0:T(8,128)S(1)}, f32[16,768,512]{2,1,0:T(8,128)}) fusion(pred[512,768]{0,1:T(8,128)(4,1)S(1)} %fusion.20, bf16[512,16,128]{2,1,0:T(8,128)(2,1)S(1)} %bitcast.73, bf16[512,16,128]{2,0,1:T(8,128)(2,1)} %copy.29, bf16[256,16,128]{2,0,1:T(8,128)(2,1)} %copy.28), kind=kOutput, calls=%fused_computation.6 | convolution fusion | flops 1635770368 | bytes 30834688 | tf_op jit(solution)/shard_map/qhd,khd->hqk/dot_general | solution.py:97
  95.6 44.3 %all-gather.5.cloned.1.call-done = bf16[32,64,2048]{2,1,0:T(8,128)(2,1)} async-done(((bf16[1,64,2048]{2,1,0:T(8,128)(2,1)}), bf16[32,64,2048]{2,1,0:T(8,128)(2,1)}) %all-gather.5.cloned.1.call-update) | async-done | bytes 8388624 | tf_op jit(solution)/shard_map/all_gather | solution.py:24
  139.9 39.1 %while.16 = (s32[]{:T(128)}, bf16[64,2048]{1,0:T(8,128)(2,1)S(1)}, bf16[64,2048]{1,0:T(8,128)(2,1)S(1)}, s32[]{:T(128)}, bf16[32,64,2048]{2,1,0:T(8,128)(2,1)}, ...) while((s32[]{:T(128)}, bf16[64,2048]{1,0:T(8,128)(2,1)S(1)}, ...), condition=%wide.region_4.5_spmd.clone, body=%wide.region_3.4_spmd.clone.sunk | while | flops 786436 | bytes 1572973 | solution.py:33
  141.1 1.2 add_select_fusion.5
  142.4 1.2 add_select_fusion.5
  143.6 1.2 add_select_fusion.5
  144.9 1.2 add_select_fusion.5
  146.2 1.2 add_select_fusion.5
  147.4 1.2 add_select_fusion.5
  149.9 1.2 add_select_fusion.5
  151.2 1.2 add_select_fusion.5
  153.7 1.2 add_select_fusion.5
  155.0 1.2 add_select_fusion.5
  157.5 1.2 add_select_fusion.5
  158.8 1.2 add_select_fusion.5
  160.0 1.2 add_select_fusion.5
  161.3 1.2 add_select_fusion.5
  162.5 1.2 add_select_fusion.5
  163.8 1.2 add_select_fusion.5
  165.1 1.2 add_select_fusion.5
  166.3 1.2 add_select_fusion.5
  167.6 1.2 add_select_fusion.5
  170.1 1.2 add_select_fusion.5
  171.4 1.2 add_select_fusion.5
  173.9 1.2 add_select_fusion.5
  175.2 1.2 add_select_fusion.5
  177.7 1.2 add_select_fusion.5
  178.9 1.5 fusion.42
  180.8 11.1 %fusion = f32[16,512]{1,0:T(8,128)S(1)} fusion(f32[16,768,512]{2,1,0:T(8,128)} %get-tuple-element.153, f32[16,512]{1,0:T(8,128)S(1)} %max.7, pred[512,768]{0,1:T(8,128)(4,1)S(1)} %fusion.20), kind=kLoop, calls=%fused_computation.5 | loop fusion | flops 25157632 | bytes 25624576 | tf_op jit(solution)/shard_map/reduce_sum | solution.py:119
  192.0 2.8 fusion.21
  194.7 14.3 %add_convert_fusion = bf16[16,128,512]{2,1,0:T(8,128)(2,1)} fusion(f32[16,128,512]{2,1,0:T(8,128)} %fusion.21, f32[16,768,512]{2,1,0:T(8,128)} %get-tuple-element.153, f32[16,512]{1,0:T(8,128)S(1)} %add.130, f32[16,512]{1,0:T(8,128)S(1)} %max.7, pred[512,768]{0,1:T(8,128)(4,1)S(1)} %fusion.20, bf16[512,16,128]{0,2,1:T(8,128)(2,1)S(1)} %bitcast.72, ...), kind=kOutput, calls=%fused_computation.12 | convolution fusion | flops 1650458624 | bytes 35061760 | tf_op jit(solution)/shard_map/hqk,khd->qhd/dot_general | solution.py:122
  209.0 188.7 %all-to-all-done = bf16[8,2048,512]{1,2,0:T(8,128)(2,1)} async-done(((bf16[8,2048,512]{1,2,0:T(8,128)(2,1)}), bf16[8,2048,512]{1,2,0:T(8,128)(2,1)}, u32[]{:S(2)}, u32[]{:S(2)}) %all-to-all-start) | async-done | bytes 16777248 | tf_op jit(solution)/shard_map/all_to_all | solution.py:14
  397.7 14.4 %fusion.3 = bf16[1,512,4096]{2,1,0:T(8,128)(2,1)} fusion(bf16[512,2048]{0,1:T(8,128)(2,1)} %bitcast.76, bf16[2048,4096]{0,1:T(8,128)(2,1)} %bitcast.15), kind=kOutput, calls=%fused_computation.9 | convolution fusion | flops 8592031744 | bytes 23068672 | tf_op jit(solution)/shard_map/dot_general | solution.py:127
  (41 shorter events, 12.9 us)
Async XLA Ops:
  6.5 3.0 copy-start
  6.5 89.1 %all-gather.3.cloned.1.call-start = ((), (), s32[]{:S(2)}) async-start(), calls=%async_computation.1 | async-start | bytes 8650752 | tf_op jit(solution)/shard_map/all_gather | solution.py:24
  8.7 0.7 copy-start.5
  9.5 130.4 %all-gather.5.cloned.1.call-start = ((), (), s32[]{:S(2)}) async-start(), calls=%async_computation.2 | async-start | bytes 8650752 | tf_op jit(solution)/shard_map/all_gather | solution.py:24
  10.0 0.7 copy-start.4
  21.5 376.2 %all-to-all-start = ((bf16[8,2048,512]{1,2,0:T(8,128)(2,1)}), bf16[8,2048,512]{1,2,0:T(8,128)(2,1)}, u32[]{:S(2)}, u32[]{:S(2)}) async-start(bf16[8,2048,512]{1,2,0:T(8,128)(2,1)} %stack.2), calls=%async_computation | async-start | bytes 33554432 | tf_op jit(solution)/shard_map/all_to_all | solution.py:14
  36.7 21.6 %collective-permute-start.1 = (bf16[256,2048]{0,1:T(8,128)(2,1)}, bf16[256,2048]{0,1:T(8,128)(2,1)}, u32[]{:S(2)}, u32[]{:S(2)}) collective-permute-start(bf16[256,2048]{0,1:T(8,128)(2,1)} %slice_bitcast_fusion), channel_id=1, source_target_pairs={{0,8},{8,16},{16,24},{24,32},{32,40},{40,48},{48,56},{56,64},{64,7... | collective-permute-start | bytes 3145736 | tf_op jit(solution)/shard_map/ppermute | solution.py:39
  41.8 39.1 %collective-permute-start = (bf16[256,2048]{1,0:T(8,128)(2,1)}, bf16[256,2048]{1,0:T(8,128)(2,1)}, u32[]{:S(2)}, u32[]{:S(2)}) collective-permute-start(bf16[256,2048]{1,0:T(8,128)(2,1)} %slice_bitcast_fusion.1), channel_id=1, source_target_pairs={{0,8},{8,16},{16,24},{24,32},{32,40},{40,48},{48,56},{56,64},{64,7... | collective-permute-start | bytes 3145736 | tf_op jit(solution)/shard_map/ppermute | solution.py:39
  46.5 3.7 copy-start.1
  52.6 30.6 %copy-start.3 = (bf16[64,8,16,128]{3,2,1,0:T(8,128)(2,1)S(1)}, bf16[64,8,16,128]{3,2,1,0:T(8,128)(2,1)}, u32[]{:S(2)}) copy-start(bf16[64,8,16,128]{3,2,1,0:T(8,128)(2,1)} %copy.39) | copy-start | bytes 6291460
  191.9 2.8 copy-start.2
Sparse Core Ops, SparseCore 0:
  9.9 67.5 all-gather.2
  80.0 59.7 all-gather.4
